TPU v7x, 32 devices: a whole 2x2x4 slice. The times are simulated.
32 devices in a mesh: grp: 1, row: 32 (over z, y, x, core).
Axes of the slice: x: 2, y: 2, z: 4, core: 2. Of those that a mesh axis runs over, the one named last changes fastest.
Arguments:
- features: bfloat16 [64, 192, 2048], P(('grp', 'row')), may hold values from -6 to 6
- branch_kernel_weight: bfloat16 [2048, 10, 128], P('row'), may hold values from -0.046875 to 0.046875
- branch_norm_bias: float32 [2, 128], replicated, may hold values from -3 to 3
- merge_weight: bfloat16 [256, 256], P('row'), may hold values from -0.375 to 0.375
- merge_bias: float32 [256], replicated, may hold values from -3 to 3
- cotangent: bfloat16 [64, 192, 256], P(('grp', 'row')), may hold values from -24 to 24
Outputs:
- merged: bfloat16 [64, 192, 256], P(('grp', 'row'))
- input_grad: bfloat16 [64, 192, 2048], P(('grp', 'row'))
- branch_kernel_gradient: float32 [2048, 10, 128], P(('grp', 'row'))
- grad_merge: float32 [256, 256], P(('grp', 'row'))
All inputs are finite; a program needn't handle non-finite values.
Results may differ from a plain program's by a relative error of at most 0.023.
The roundings to bfloat16 on the way count: a program that leaves them out, or rounds other values in their place, can miss the bound.
Values may be sent and summed in bfloat16 or wider, within the bound.
No kernel may reach another device: no remote copies, remote signals or barrier semaphores. Data moves between devices by JAX's collectives and lax.ppermute only.
A program may use at most 128 MiB of HBM per device.

v0:
```python
import math
import jax
import jax.numpy as jnp
from jax import lax
from jax.sharding import PartitionSpec as P

DILATION_RATE = 18


def passed_along(block, axis, distance):
    devices = range(lax.axis_size(axis))
    route = [(i - distance, i) for i in devices if i - distance in devices]
    return lax.ppermute(block, axis, route)


def transposed_product(left, right):
    return lax.dot_general(
        left, right, (((0,), (0,)), ((), ())), preferred_element_type=jnp.float32
    )


def ndot(left, right):
    return lax.dot_general(
        left, right, (((1,), (1,)), ((), ())), preferred_element_type=jnp.float32
    )


def gather_feature_rows(row_block, device_step):
    return passed_along(row_block, "row", device_step)


def gather_gradient_rows(row_block, device_step):
    return passed_along(row_block, "row", device_step)


def load_row_block(row_block, row_offset, pull_rows):
    block_row_count = row_block.shape[0]
    device_off, inner_off = divmod(row_offset, block_row_count)
    return pull_rows(row_block, -device_off)


def on_device(
    features, branch_kernel_weight, branch_norm_bias, merge_weight, merge_bias, cotangent
):
    block_row_count = features.shape[0]
    width_columns = features.shape[1]
    channel_count = features.shape[2]
    branch_channel_width = branch_kernel_weight.shape[2]
    pixel_count = block_row_count * width_columns
    gradient_scale = 1.0 / math.sqrt(block_row_count * lax.axis_size("row") * width_columns)
    flattened = features.reshape(pixel_count, channel_count)
    row_groups = [
        load_row_block(features, -DILATION_RATE, gather_feature_rows),
        features,
        load_row_block(features, DILATION_RATE, gather_feature_rows),
    ]
    padded_row_groups = [
        jnp.pad(row_group, ((0, 0), (DILATION_RATE, DILATION_RATE), (0, 0)))
        for row_group in row_groups
    ]
    tap_windows = [
        padded_row_groups[tap_number // 3][
            :, tap_number % 3 * DILATION_RATE : tap_number % 3 * DILATION_RATE + width_columns
        ].reshape(pixel_count, channel_count)
        for tap_number in range(9)
    ]
    whole_branch, whole_merge = (
        lax.all_gather(branch_kernel_weight, "row", axis=0, tiled=True),
        lax.all_gather(merge_weight, "row", axis=0, tiled=True),
    )
    z_one = jnp.dot(flattened, whole_branch[:, 0, :], preferred_element_type=jnp.float32)
    dilated_preactivation = jnp.zeros((pixel_count, branch_channel_width), jnp.float32)
    for tap_number in range(9):
        dilated_preactivation = dilated_preactivation + jnp.dot(
            tap_windows[tap_number],
            whole_branch[:, 1 + tap_number, :],
            preferred_element_type=jnp.float32,
        )
    pointwise_activation = jnp.maximum(z_one + branch_norm_bias[0], 0.0).astype(jnp.bfloat16)
    dilated_activation = jnp.maximum(dilated_preactivation + branch_norm_bias[1], 0.0).astype(
        jnp.bfloat16
    )
    combined = jnp.concatenate([pointwise_activation, dilated_activation], axis=1)
    merged = jnp.maximum(
        jnp.dot(combined, whole_merge, preferred_element_type=jnp.float32) + merge_bias, 0.0
    ).astype(jnp.bfloat16)
    grad_out = jnp.where(
        merged > 0, cotangent.reshape(pixel_count, merged.shape[1]), jnp.zeros((), jnp.bfloat16)
    )
    grad_merge = (
        lax.psum_scatter(
            transposed_product(combined, grad_out), "row", scatter_dimension=0, tiled=True
        )
        * gradient_scale
    )
    backward_pass = ndot(grad_out, whole_merge)
    pointwise_gradient = jnp.where(
        pointwise_activation > 0, backward_pass[:, :branch_channel_width], 0.0
    ).astype(jnp.bfloat16)
    dilated_gradient = jnp.where(
        dilated_activation > 0, backward_pass[:, branch_channel_width:], 0.0
    ).astype(jnp.bfloat16)
    gradient_map = dilated_gradient.reshape(block_row_count, width_columns, branch_channel_width)
    gradient_row_groups = [
        load_row_block(gradient_map, DILATION_RATE, gather_gradient_rows),
        gradient_map,
        load_row_block(gradient_map, -DILATION_RATE, gather_gradient_rows),
    ]
    padded_gradient = [
        jnp.pad(gradient_row_group, ((0, 0), (DILATION_RATE, DILATION_RATE), (0, 0)))
        for gradient_row_group in gradient_row_groups
    ]
    grad_views = [
        padded_gradient[tap_number // 3][
            :,
            (2 - tap_number % 3) * DILATION_RATE : (2 - tap_number % 3) * DILATION_RATE
            + width_columns,
        ].reshape(pixel_count, branch_channel_width)
        for tap_number in range(9)
    ]
    pieces_list = [transposed_product(flattened, pointwise_gradient)]
    for branch_tap_number in range(9):
        pieces_list.append(transposed_product(tap_windows[branch_tap_number], dilated_gradient))
    branch_kernel_gradient = (
        lax.psum_scatter(jnp.stack(pieces_list, axis=1), "row", scatter_dimension=0, tiled=True)
        * gradient_scale
    )
    input_total = ndot(pointwise_gradient, whole_branch[:, 0, :])
    for tap_number in range(9):
        input_total = input_total + ndot(grad_views[tap_number], whole_branch[:, 1 + tap_number, :])
    input_grad = input_total.astype(jnp.bfloat16).reshape(
        block_row_count, width_columns, channel_count
    )
    return (
        merged.reshape(block_row_count, width_columns, merged.shape[1]),
        input_grad,
        branch_kernel_gradient,
        grad_merge,
    )


def solution(mesh):
    placed = (
        P(("grp", "row"), None, None),
        P("row", None, None),
        P(),
        P("row", None),
        P(),
        P(("grp", "row"), None, None),
    )
    return jax.shard_map(
        on_device,
        mesh=mesh,
        in_specs=placed,
        out_specs=(
            P(("grp", "row"), None, None),
            P(("grp", "row"), None, None),
            P(("grp", "row"), None, None),
            P(("grp", "row"), None),
        ),
        check_vma=False,
    )
```

profile of v0, /device:TPU:14, one launch (start us, length us, event | category | flops | bytes accessed | tf_op | source)
XLA Modules:
  0.0 479.6 jit_solution(15988764721342532943)
XLA Ops:
  7.9 2.9 collective-permute-start
  10.9 3.6 collective-permute-start.1
  14.5 101.5 %all_gather.7 = bf16[256,256]{1,0:T(8,128)(2,1)S(1)} all-gather(bf16[8,256]{1,0:T(8,128)(2,1)} %param.9), channel_id=1, replica_groups=mesh['grp'=1,'row'=32] {'row'}, dimensions={0}, use_global_device_ids=true | all-gather | bytes 135168 | tf_op jit(solution)/shard_map/all_gather | solution.py:69
  116.8 4.3 pad_slice_fusion.2
  121.2 2.3 pad_slice_fusion.5
  123.5 1.8 pad_slice_fusion.1
  125.3 2.7 fusion.26
  128.0 2.5 fusion.28
  130.6 1.7 fusion.24
  141.4 3.0 fusion.5
  147.2 1.5 fusion.3
  151.6 1.5 fusion.1
  156.3 17.6 %copy.65 = f32[2048,10,128]{2,1,0:T(8,128)} copy(f32[2048,10,128]{0,2,1:T(8,128)} %fusion) | data formatting | bytes 20971520 | tf_op jit(solution)/shard_map/stack | solution.py:125
  174.0 1.9 collective-permute-start.2
  175.9 3.6 collective-permute-start.3
  179.6 1.8 fusion.29
  181.4 1.7 fusion.27
  183.1 3.3 fusion.21
  188.3 2.3 fusion.31
  190.6 2.3 fusion.23
  192.8 2.3 fusion.32
  195.1 8.0 %add_convert_fusion = bf16[384,2048]{1,0:T(8,128)(2,1)} fusion(f32[384,2048]{1,0:T(8,128)} %fusion.32, f32[384,2048]{1,0:T(8,128)} %fusion.31, f32[384,2048]{1,0:T(8,128)S(1)} %fusion.30, f32[384,2048]{1,0:T(8,128)S(1)} %fusion.29, f32[384,2048]{1,0:T(8,128)S(1)} %fusion.27, f32[384,2048]{1,0:T(8,128)S(1)} %fusion.25, f32[384,2048]{1,0:T(8,128)} %fusion.23, ...), kind=kOutput, calls=%fused_computation | convolution fusion | flops 209190912 | bytes 30507008 | tf_op jit(solution)/shard_map/dot_general | solution.py:23
  203.1 52.5 %reduce-scatter.5.cloned.1.call-done = f32[8,256]{1,0:T(8,128)} async-done(((f32[256,256]{1,0:T(8,128)}), f32[8,256]{1,0:T(8,128)}) %reduce-scatter.5.cloned.1.call-update) | async-done | bytes 8208 | tf_op jit(solution)/shard_map/reduce_scatter | solution.py:91
  256.8 214.3 %reduce-scatter.3.cloned.1.call-done = f32[64,10,128]{2,1,0:T(8,128)} async-done(((f32[2048,10,128]{2,1,0:T(8,128)}), f32[64,10,128]{2,1,0:T(8,128)}) %reduce-scatter.3.cloned.1.call-update) | async-done | bytes 327696 | tf_op jit(solution)/shard_map/reduce_scatter | solution.py:125
  (79 shorter events, 24.5 us)
Async XLA Ops:
  7.2 118.1 %all-gather.2.cloned.1.call-start = ((), (), s32[]{:S(2)}) async-start(), calls=%async_computation.2 | async-start | bytes 5406720 | tf_op jit(solution)/shard_map/all_gather | solution.py:68
  7.9 247.6 %reduce-scatter.5.cloned.1.call-start = ((), (), s32[]{:S(2)}) async-start(), calls=%async_computation.4 | async-start | bytes 270336 | tf_op jit(solution)/shard_map/reduce_scatter | solution.py:91
  7.9 113.2 %collective-permute-start = (bf16[2,192,2048]{2,1,0:T(8,128)(2,1)}, bf16[2,192,2048]{2,1,0:T(8,128)(2,1)S(1)}, u32[]{:S(2)}, u32[]{:S(2)}) collective-permute-start(bf16[2,192,2048]{2,1,0:T(8,128)(2,1)} %param.6), channel_id=1, source_target_pairs={{0,9},{1,10},{2,11},{3,12},{4,13},{5,14},{6,15},{7,16},{8,17},{9,1... | collective-permute-start | bytes 4718600 | tf_op jit(solution)/shard_map/ppermute | solution.py:13
  10.9 112.6 %collective-permute-start.1 = (bf16[2,192,2048]{2,1,0:T(8,128)(2,1)}, bf16[2,192,2048]{2,1,0:T(8,128)(2,1)S(1)}, u32[]{:S(2)}, u32[]{:S(2)}) collective-permute-start(bf16[2,192,2048]{2,1,0:T(8,128)(2,1)} %param.6), channel_id=1, source_target_pairs={{9,0},{10,1},{11,2},{12,3},{13,4},{14,5},{15,6},{16,7},{17,8},{18,... | collective-permute-start | bytes 4718600 | tf_op jit(solution)/shard_map/ppermute | solution.py:13
  116.1 20.8 %copy-start.14 = (bf16[256,256]{1,0:T(8,128)(2,1)}, bf16[256,256]{1,0:T(8,128)(2,1)S(1)}, u32[]{:S(2)}) copy-start(bf16[256,256]{1,0:T(8,128)(2,1)S(1)} %all_gather.7) | copy-start | bytes 393220
  121.1 2.3 copy-start.4
  125.3 7.0 %copy-start.2 = (bf16[2,192,2048]{2,1,0:T(8,128)(2,1)}, bf16[2,192,2048]{2,1,0:T(8,128)(2,1)S(1)}, u32[]{:S(2)}) copy-start(bf16[2,192,2048]{2,1,0:T(8,128)(2,1)S(1)} %get-tuple-element.17) | copy-start | bytes 4718596
  125.3 5.3 %copy-start.5 = (bf16[2,192,2048]{2,1,0:T(8,128)(2,1)S(1)}, bf16[2,192,2048]{2,1,0:T(8,128)(2,1)}, u32[]{:S(2)}) copy-start(bf16[2,192,2048]{2,1,0:T(8,128)(2,1)} %copy-done.4) | copy-start | bytes 4718596
  125.3 7.0 %copy-start.1 = (bf16[2048,10,128]{2,0,1:T(8,128)(2,1)S(1)}, bf16[2048,10,128]{2,0,1:T(8,128)(2,1)}, u32[]{:S(2)}) copy-start(bf16[2048,10,128]{2,0,1:T(8,128)(2,1)} %all-gather.2.cloned.1.call-done) | copy-start | bytes 15728644
  130.6 3.0 copy-start.13
  133.0 1.4 copy-start
  133.6 2.0 copy-start.7
  134.4 1.9 copy-start.10
  141.4 3.0 copy-start.6
  141.4 4.4 copy-start.12
  144.3 2.9 copy-start.9
  147.2 2.9 copy-start.8
  148.7 2.9 copy-start.11
  151.6 3.3 copy-start.3
  153.1 318.0 %reduce-scatter.3.cloned.1.call-start = ((), (), s32[]{:S(2)}) async-start(), calls=%async_computation.3 | async-start | bytes 17301504 | tf_op jit(solution)/shard_map/reduce_scatter | solution.py:125
  174.0 13.0 %collective-permute-start.2 = (bf16[2,192,128]{2,1,0:T(8,128)(2,1)S(1)}, bf16[2,192,128]{2,1,0:T(8,128)(2,1)S(1)}, u32[]{:S(2)}, u32[]{:S(2)}) collective-permute-start(bf16[2,192,128]{2,1,0:T(8,128)(2,1)S(1)} %bitcast.182), channel_id=1, source_target_pairs={{9,0},{10,1},{11,2},{12,3},{13,4},{14,5},{15,6},{16,7},{17,8},{18,... | collective-permute-start | bytes 294920 | tf_op jit(solution)/shard_map/ppermute | solution.py:13
  175.9 11.1 %collective-permute-start.3 = (bf16[2,192,128]{2,1,0:T(8,128)(2,1)S(1)}, bf16[2,192,128]{2,1,0:T(8,128)(2,1)S(1)}, u32[]{:S(2)}, u32[]{:S(2)}) collective-permute-start(bf16[2,192,128]{2,1,0:T(8,128)(2,1)S(1)} %bitcast.183), channel_id=1, source_target_pairs={{0,9},{1,10},{2,11},{3,12},{4,13},{5,14},{6,15},{7,16},{8,17},{9,1... | collective-permute-start | bytes 294920 | tf_op jit(solution)/shard_map/ppermute | solution.py:13
  179.6 6.8 %slice-start = ((s8[5242880]{0:T(1024)(128)(4,1)}), s8[4194304]{0:T(1024)(128)(4,1)S(1)}, s32[]{:S(2)}) async-start(s8[5242880]{0:T(1024)(128)(4,1)} %bitcast.162), calls=%async_computation.5 | async-start | bytes 8388608
  181.4 5.0 %slice-start.1 = ((s8[5242880]{0:T(1024)(128)(4,1)}), s8[1048576]{0:T(1024)(128)(4,1)S(1)}, s32[]{:S(2)}) async-start(s8[5242880]{0:T(1024)(128)(4,1)} %bitcast.162), calls=%async_computation.6 | async-start | bytes 2097152
  (2 other events, 2.5 us)
Sparse Core Ops, SparseCore 0:
  10.9 78.9 all-gather.1
  153.3 102.2 reduce-scatter.4
  257.9 213.1 reduce-scatter.2
where the time goes:
time: 480 us
  waiting for transfers between devices  268 us (56%)
  blocking collectives  102 us (21%)
  matrix products  53.5 us (11%)
  local copies, waits for them, and re-layouts  28.1 us (6%)
  between operations  14.1 us (3%)
  starting transfers between devices  12.4 us (3%)
    reduce_scatter x1, waiting for transfers between devices, on_device(): lax.psum_scatter(jnp.stack(pieces_list, axis=1), 'row', scatter_dimension...  214 us
    all_gather x1, blocking collectives, on_device(): lax.all_gather(merge_weight, 'row', axis=0, tiled=True)  102 us
    reduce_scatter x1, waiting for transfers between devices, on_device(): lax.psum_scatter(transposed_product(combined, grad_out), 'row', scatter_d...  52.5 us
    dot_general x11, matrix products, ndot(): lax.dot_general(left, right, (((1,), (1,)), ((), ())), preferred_element_...  24.4 us
    another operation x1, local copies, waits for them, and re-layouts, on_device(): jnp.stack(pieces_list, axis=1)  17.6 us
    dot_general x11, matrix products, transposed_product(): lax.dot_general(left, right, (((0,), (0,)), ((), ())), preferred_element_...  16.9 us
    ppermute x4, starting transfers between devices, passed_along(): return lax.ppermute(block, axis, route)  12.1 us
    dot_general x9, matrix products, on_device(): jnp.dot(tap_windows[tap_number], whole_branch[:, 1 + tap_number, :], pref...  10.6 us
  transfers between devices with their start and end apart: 7, of which 2 were waited for; matrix products, arithmetic and copies ran while one was open for 11% of the time, Pallas kernels for 0%

commit v1 on v0

--- a/solution.py
+++ b/solution.py
@@ -1,3 +1,4 @@
+import functools
 import math
 import jax
 import jax.numpy as jnp
@@ -5,6 +6,23 @@
 from jax.sharding import PartitionSpec as P
 
 DILATION_RATE = 18
+
+
+def _group_matrix(content, device_axis):
+    wide_out, u_next = (lax.axis_size(device_axis), lax.axis_index(device_axis))
+    lower, d_next = (content, 1)
+    while d_next < wide_out:
+        left_arr = lax.ppermute(
+            lower, axis_name=device_axis, perm=[(at, at ^ d_next) for at in range(wide_out)]
+        )
+        n_now = jnp.concatenate([lower, left_arr], axis=0)
+        block_last = jnp.concatenate([left_arr, lower], axis=0)
+        lower = jnp.where(u_next & d_next == 0, n_now, block_last)
+        d_next = 2 * d_next
+    return lower
+
+
+perform_matrix = functools.partial(_group_matrix, device_axis="row")
 
 
 def passed_along(block, axis, distance):
@@ -66,7 +84,7 @@
     ]
     whole_branch, whole_merge = (
         lax.all_gather(branch_kernel_weight, "row", axis=0, tiled=True),
-        lax.all_gather(merge_weight, "row", axis=0, tiled=True),
+        perform_matrix(merge_weight),
     )
     z_one = jnp.dot(flattened, whole_branch[:, 0, :], preferred_element_type=jnp.float32)
     dilated_preactivation = jnp.zeros((pixel_count, branch_channel_width), jnp.float32)

time: 480 us -> 451 us (0.940)
  blocking collectives: 102 us -> 0 us
  waiting for transfers between devices: 268 us -> 336 us
    all_gather x1 -> x0, blocking collectives: 102 us -> none  [on_device(): lax.all_gather(merge_weight, 'row', axis=0, tiled=True)]
    ppermute x0 -> x5, waiting for transfers between devices: none -> 38 us  [_group_matrix(): lax.ppermute(lower, axis_name=device_axis, perm=[(at, at ^ d_next) for at...]
    ppermute x4, waiting for transfers between devices: 0.01 us -> 27.9 us  [passed_along(): return lax.ppermute(block, axis, route)]
  transfers between devices with their start and end apart: 7 -> 12, of which waited for: 2 -> 6; matrix products, arithmetic and copies ran while one was open for 11% -> 15% of each run, Pallas kernels for 0% -> 0%
where the time goes in v1:
time: 451 us; the launch traced here: 450 us
  waiting for transfers between devices  336 us (75%)
  matrix products  52.9 us (12%)
  local copies, waits for them, and re-layouts  28 us (6%)
  starting transfers between devices  15.6 us (3%)
  between operations  14.1 us (3%)
    reduce_scatter x1, waiting for transfers between devices, on_device(): lax.psum_scatter(jnp.stack(pieces_list, axis=1), 'row', scatter_dimension...  214 us
    reduce_scatter x1, waiting for transfers between devices, on_device(): lax.psum_scatter(transposed_product(combined, grad_out), 'row', scatter_d...  55.2 us
    ppermute x5, waiting for transfers between devices, _group_matrix(): lax.ppermute(lower, axis_name=device_axis, perm=[(at, at ^ d_next) for at...  38 us
    ppermute x4, waiting for transfers between devices, passed_along(): return lax.ppermute(block, axis, route)  27.9 us
    dot_general x11, matrix products, ndot(): lax.dot_general(left, right, (((1,), (1,)), ((), ())), preferred_element_...  24.4 us
    another operation x1, local copies, waits for them, and re-layouts, on_device(): jnp.stack(pieces_list, axis=1)  17.6 us
    dot_general x11, matrix products, transposed_product(): lax.dot_general(left, right, (((0,), (0,)), ((), ())), preferred_element_...  16.9 us
    ppermute x4, starting transfers between devices, passed_along(): return lax.ppermute(block, axis, route)  12.1 us
  transfers between devices with their start and end apart: 12, of which 6 were waited for; matrix products, arithmetic and copies ran while one was open for 15% of the time, Pallas kernels for 0%

profile of v1, /device:TPU:14, one launch (start us, length us, event | category | flops | bytes accessed | tf_op | source)
XLA Modules:
  0.0 449.9 jit_solution(12066763118177373410)
XLA Ops:
  8.0 2.9 collective-permute-start
  10.9 3.6 collective-permute-start.1
  18.2 5.6 %collective-permute-done.3 = bf16[16,256]{1,0:T(8,128)(2,1)S(1)} collective-permute-done((bf16[16,256]{1,0:T(8,128)(2,1)S(1)}, bf16[16,256]{1,0:T(8,128)(2,1)S(1)}, u32[]{:S(2)}, u32[]{:S(2)}) %collective-permute-start.3) | collective-permute-done | bytes 8224 | tf_op jit(solution)/shard_map/ppermute | solution.py:15
  23.8 4.3 pad_slice_fusion.2
  28.2 31.1 %collective-permute-done.5 = bf16[64,256]{1,0:T(8,128)(2,1)S(1)} collective-permute-done((bf16[64,256]{1,0:T(8,128)(2,1)S(1)}, bf16[64,256]{1,0:T(8,128)(2,1)S(1)}, u32[]{:S(2)}, u32[]{:S(2)}) %collective-permute-start.5) | collective-permute-done | bytes 32800 | tf_op jit(solution)/shard_map/ppermute | solution.py:15
  60.9 27.8 %collective-permute-done = bf16[2,192,2048]{2,1,0:T(8,128)(2,1)S(1)} collective-permute-done((bf16[2,192,2048]{2,1,0:T(8,128)(2,1)}, bf16[2,192,2048]{2,1,0:T(8,128)(2,1)S(1)}, u32[]{:S(2)}, u32[]{:S(2)}) %collective-permute-start) | collective-permute-done | bytes 1572896 | tf_op jit(solution)/shard_map/ppermute | solution.py:31
  88.8 2.3 pad_slice_fusion.5
  91.1 2.3 pad_slice_fusion.1
  93.4 2.2 fusion.26
  95.6 2.5 fusion.28
  98.1 1.7 fusion.24
  109.1 3.0 fusion.5
  123.9 17.6 %copy.65 = f32[2048,10,128]{2,1,0:T(8,128)} copy(f32[2048,10,128]{0,2,1:T(8,128)} %fusion) | data formatting | bytes 20971520 | tf_op jit(solution)/shard_map/stack | solution.py:143
  141.7 1.9 collective-permute-start.7
  143.6 3.6 collective-permute-start.8
  147.3 1.8 fusion.29
  149.1 1.7 fusion.27
  150.8 3.3 fusion.21
  156.0 2.3 fusion.31
  158.2 2.3 fusion.23
  160.5 2.3 fusion.32
  162.8 8.0 %add_convert_fusion = bf16[384,2048]{1,0:T(8,128)(2,1)} fusion(f32[384,2048]{1,0:T(8,128)} %fusion.32, f32[384,2048]{1,0:T(8,128)} %fusion.31, f32[384,2048]{1,0:T(8,128)S(1)} %fusion.30, f32[384,2048]{1,0:T(8,128)S(1)} %fusion.29, f32[384,2048]{1,0:T(8,128)S(1)} %fusion.27, f32[384,2048]{1,0:T(8,128)S(1)} %fusion.25, f32[384,2048]{1,0:T(8,128)} %fusion.23, ...), kind=kOutput, calls=%fused_computation | convolution fusion | flops 209190912 | bytes 30507008 | tf_op jit(solution)/shard_map/dot_general | solution.py:41
  170.7 55.2 %reduce-scatter.5.cloned.1.call-done = f32[8,256]{1,0:T(8,128)} async-done(((f32[256,256]{1,0:T(8,128)}), f32[8,256]{1,0:T(8,128)}) %reduce-scatter.5.cloned.1.call-update) | async-done | bytes 8208 | tf_op jit(solution)/shard_map/reduce_scatter | solution.py:109
  227.2 214.2 %reduce-scatter.3.cloned.1.call-done = f32[64,10,128]{2,1,0:T(8,128)} async-done(((f32[2048,10,128]{2,1,0:T(8,128)}), f32[64,10,128]{2,1,0:T(8,128)}) %reduce-scatter.3.cloned.1.call-update) | async-done | bytes 327696 | tf_op jit(solution)/shard_map/reduce_scatter | solution.py:143
  (92 shorter events, 32.3 us)
Async XLA Ops:
  7.2 21.0 %copy-start.13 = (f32[2,128]{1,0:T(2,128)S(1)}, f32[2,128]{1,0:T(2,128)}, u32[]{:S(2)}) copy-start(f32[2,128]{1,0:T(2,128)} %param.8) | copy-start | bytes 3076
  7.2 86.2 %all-gather.2.cloned.1.call-start = ((), (), s32[]{:S(2)}) async-start(), calls=%async_computation.2 | async-start | bytes 5406720 | tf_op jit(solution)/shard_map/all_gather | solution.py:86
  7.9 218.0 %reduce-scatter.5.cloned.1.call-start = ((), (), s32[]{:S(2)}) async-start(), calls=%async_computation.4 | async-start | bytes 270336 | tf_op jit(solution)/shard_map/reduce_scatter | solution.py:109
  8.0 80.8 %collective-permute-start = (bf16[2,192,2048]{2,1,0:T(8,128)(2,1)}, bf16[2,192,2048]{2,1,0:T(8,128)(2,1)S(1)}, u32[]{:S(2)}, u32[]{:S(2)}) collective-permute-start(bf16[2,192,2048]{2,1,0:T(8,128)(2,1)} %param.6), channel_id=1, source_target_pairs={{0,9},{1,10},{2,11},{3,12},{4,13},{5,14},{6,15},{7,16},{8,17},{9,1... | collective-permute-start | bytes 4718600 | tf_op jit(solution)/shard_map/ppermute | solution.py:31
  10.9 80.2 %collective-permute-start.1 = (bf16[2,192,2048]{2,1,0:T(8,128)(2,1)}, bf16[2,192,2048]{2,1,0:T(8,128)(2,1)S(1)}, u32[]{:S(2)}, u32[]{:S(2)}) collective-permute-start(bf16[2,192,2048]{2,1,0:T(8,128)(2,1)} %param.6), channel_id=1, source_target_pairs={{9,0},{10,1},{11,2},{12,3},{13,4},{14,5},{15,6},{16,7},{17,8},{18,... | collective-permute-start | bytes 4718600 | tf_op jit(solution)/shard_map/ppermute | solution.py:31
  14.5 1.4 collective-permute-start.2
  16.7 7.0 %collective-permute-start.3 = (bf16[16,256]{1,0:T(8,128)(2,1)S(1)}, bf16[16,256]{1,0:T(8,128)(2,1)S(1)}, u32[]{:S(2)}, u32[]{:S(2)}) collective-permute-start(bf16[16,256]{1,0:T(8,128)(2,1)S(1)} %maximum_select_fusion.6), channel_id=1, source_target_pairs={{0,2},{1,3},{2,0},{3,1},{4,6},{5,7},{6,4},{7,5},{8,10},{9,11},{10,... | collective-permute-start | bytes 24584 | tf_op jit(solution)/shard_map/ppermute | solution.py:15
  23.8 4.3 collective-permute-start.4
  28.1 31.2 %collective-permute-start.5 = (bf16[64,256]{1,0:T(8,128)(2,1)S(1)}, bf16[64,256]{1,0:T(8,128)(2,1)S(1)}, u32[]{:S(2)}, u32[]{:S(2)}) collective-permute-start(bf16[64,256]{1,0:T(8,128)(2,1)S(1)} %maximum_select_fusion.2), channel_id=1, source_target_pairs={{0,8},{1,9},{2,10},{3,11},{4,12},{5,13},{6,14},{7,15},{8,0},{9,1},... | collective-permute-start | bytes 98312 | tf_op jit(solution)/shard_map/ppermute | solution.py:15
  59.3 45.2 %collective-permute-start.6 = (bf16[128,256]{1,0:T(8,128)(2,1)S(1)}, bf16[128,256]{1,0:T(8,128)(2,1)S(1)}, u32[]{:S(2)}, u32[]{:S(2)}) collective-permute-start(bf16[128,256]{1,0:T(8,128)(2,1)S(1)} %maximum_select_fusion.1), channel_id=1, source_target_pairs={{0,16},{1,17},{2,18},{3,19},{4,20},{5,21},{6,22},{7,23},{8,24},{9,... | collective-permute-start | bytes 196616 | tf_op jit(solution)/shard_map/ppermute | solution.py:15
  88.8 9.4 %copy-start.2 = (bf16[2,192,2048]{2,1,0:T(8,128)(2,1)}, bf16[2,192,2048]{2,1,0:T(8,128)(2,1)S(1)}, u32[]{:S(2)}) copy-start(bf16[2,192,2048]{2,1,0:T(8,128)(2,1)S(1)} %collective-permute-done) | copy-start | bytes 4718596
  93.4 6.5 %copy-start.1 = (bf16[2048,10,128]{2,0,1:T(8,128)(2,1)S(1)}, bf16[2048,10,128]{2,0,1:T(8,128)(2,1)}, u32[]{:S(2)}) copy-start(bf16[2048,10,128]{2,0,1:T(8,128)(2,1)} %all-gather.2.cloned.1.call-done) | copy-start | bytes 15728644
  93.4 6.5 %copy-start.7 = (bf16[2,192,2048]{2,1,0:T(8,128)(2,1)S(1)}, bf16[2,192,2048]{2,1,0:T(8,128)(2,1)}, u32[]{:S(2)}) copy-start(bf16[2,192,2048]{2,1,0:T(8,128)(2,1)} %get-tuple-element.17) | copy-start | bytes 4718596
  98.1 3.0 copy-start.12
  109.1 3.0 copy-start.3
  109.1 4.4 copy-start.11
  112.0 2.9 copy-start.6
  114.9 2.9 copy-start.5
  119.3 3.2 copy-start.8
  120.9 320.6 %reduce-scatter.3.cloned.1.call-start = ((), (), s32[]{:S(2)}) async-start(), calls=%async_computation.3 | async-start | bytes 17301504 | tf_op jit(solution)/shard_map/reduce_scatter | solution.py:143
  141.7 13.0 %collective-permute-start.7 = (bf16[2,192,128]{2,1,0:T(8,128)(2,1)S(1)}, bf16[2,192,128]{2,1,0:T(8,128)(2,1)S(1)}, u32[]{:S(2)}, u32[]{:S(2)}) collective-permute-start(bf16[2,192,128]{2,1,0:T(8,128)(2,1)S(1)} %bitcast.180), channel_id=1, source_target_pairs={{9,0},{10,1},{11,2},{12,3},{13,4},{14,5},{15,6},{16,7},{17,8},{18,... | collective-permute-start | bytes 294920 | tf_op jit(solution)/shard_map/ppermute | solution.py:31
  143.6 11.2 %collective-permute-start.8 = (bf16[2,192,128]{2,1,0:T(8,128)(2,1)S(1)}, bf16[2,192,128]{2,1,0:T(8,128)(2,1)S(1)}, u32[]{:S(2)}, u32[]{:S(2)}) collective-permute-start(bf16[2,192,128]{2,1,0:T(8,128)(2,1)S(1)} %bitcast.181), channel_id=1, source_target_pairs={{0,9},{1,10},{2,11},{3,12},{4,13},{5,14},{6,15},{7,16},{8,17},{9,1... | collective-permute-start | bytes 294920 | tf_op jit(solution)/shard_map/ppermute | solution.py:31
  147.3 6.8 %slice-start = ((s8[5242880]{0:T(1024)(128)(4,1)}), s8[4194304]{0:T(1024)(128)(4,1)S(1)}, s32[]{:S(2)}) async-start(s8[5242880]{0:T(1024)(128)(4,1)} %bitcast.160), calls=%async_computation.5 | async-start | bytes 8388608
  149.1 5.0 %slice-start.1 = ((s8[5242880]{0:T(1024)(128)(4,1)}), s8[1048576]{0:T(1024)(128)(4,1)S(1)}, s32[]{:S(2)}) async-start(s8[5242880]{0:T(1024)(128)(4,1)} %bitcast.160), calls=%async_computation.6 | async-start | bytes 2097152
  (7 other events, 12.2 us)
Sparse Core Ops, SparseCore 0:
  10.9 79.3 all-gather.1
  121.0 104.8 reduce-scatter.4
  228.3 213.0 reduce-scatter.2
